TPU v7x, 512 devices: a whole 4x8x8 slice. The times are simulated.
512 devices in a mesh: prow: 16 (over y, core), pcol: 32 (over z, x).
Axes of the slice: x: 4, y: 8, z: 8, core: 2. Of those that a mesh axis runs over, the one named last changes fastest.
Arguments:
- matrix: bfloat16 [2, 16, 512, 2, 32, 512], P(None, 'prow', None, None, 'pcol'), may hold values from -6 to 6
- pivots: int32 [2, 512], replicated, may hold values from 0 to 16383, as said below
- lower_inverse: bfloat16 [2, 512, 512], replicated, as said below
- upper_inverse: bfloat16 [2, 512, 512], replicated, as said below
Outputs:
- factored: bfloat16 [2, 16, 512, 2, 32, 512], P(None, 'prow', None, None, 'pcol')
Inputs may be any that keep to these rules, and one draw needn't show every extreme that they name: Each row of pivots holds 512 distinct row indices; those of panel k are k * 512 or more. lower_inverse[k] is unit lower triangular. upper_inverse[k] is upper triangular with a positive diagonal.
All inputs are finite; a program needn't handle non-finite values.
Results may differ from a plain program's by a relative error of at most 0.0084.
Values may be sent and summed in bfloat16 or wider, within the bound.
A program may use at most 64 MiB of HBM per device.

v0:
```python
import jax
import jax.numpy as jnp
from jax import lax
from jax.sharding import PartitionSpec as P

PANELS = 2


def from_root(value, axis, root):
    mine = lax.axis_index(axis) == root
    return lax.psum(jnp.where(mine, value, jnp.zeros_like(value)), axis)


def pairing(sources, first_row, panel_width):
    top_ids = first_row + jnp.arange(panel_width, dtype=jnp.int32)
    chosen = jnp.any(sources[None, :] == top_ids[:, None], axis=1)
    leftover = jnp.logical_not(chosen)
    left_rank = jnp.cumsum(leftover.astype(jnp.int32)) - 1
    vacated = sources >= first_row + panel_width
    vac_rank = jnp.cumsum(vacated.astype(jnp.int32)) - 1
    match_table = leftover[None, :] & (left_rank[None, :] == vac_rank[:, None])
    receive = jnp.sum(jnp.where(match_table, top_ids[None, :], 0), axis=1)
    return (receive, vacated)


def per_device(matrix, pivots, lower_inverse, upper_inverse):
    shape_in = matrix.shape
    row_blocks = shape_in[0]
    block_size = shape_in[2]
    col_blocks = shape_in[3]
    local_tile = matrix.reshape(row_blocks * block_size, col_blocks * block_size)
    prow_count = lax.axis_size("prow")
    pcol_count = lax.axis_size("pcol")
    prow_index = lax.axis_index("prow")
    pcol_index = lax.axis_index("pcol")
    local_rows = jnp.arange(row_blocks * block_size, dtype=jnp.int32)
    rows_global = (
        local_rows // block_size * prow_count + prow_index
    ) * block_size + local_rows % block_size
    local_cols = jnp.arange(col_blocks * block_size, dtype=jnp.int32)
    cols_global = (
        local_cols // block_size * pcol_count + pcol_index
    ) * block_size + local_cols % block_size
    for step_index in range(PANELS):
        first_row = step_index * block_size
        past_row = first_row + block_size
        sources = pivots[step_index]
        receive, vacated = pairing(sources, first_row, block_size)
        src_block = sources // block_size
        owner_row = src_block % prow_count
        src_local = src_block // prow_count * block_size + sources % block_size
        owned_row = owner_row == prow_index
        picked = jnp.take(local_tile, jnp.where(owned_row, src_local, 0), axis=0)
        contrib = jnp.where(owned_row[:, None], picked, jnp.zeros_like(picked))
        diag_row = step_index % prow_count
        diag_local = step_index // prow_count
        own_top = local_tile[diag_local * block_size : (diag_local + 1) * block_size]
        old_top = from_root(own_top, "prow", diag_row)
        hit_table = (rows_global[:, None] == sources[None, :]) & vacated[None, :]
        hit_rows = jnp.any(hit_table, axis=1)
        giver_row = jnp.sum(jnp.where(hit_table, receive[None, :] - first_row, 0), axis=1)
        local_tile = jnp.where(hit_rows[:, None], jnp.take(old_top, giver_row, axis=0), local_tile)
        cols_right = cols_global >= past_row
        top_rows = lax.psum(contrib, "prow").astype(jnp.float32).astype(jnp.bfloat16)
        upper_rows = jnp.dot(
            lower_inverse[step_index], top_rows, preferred_element_type=jnp.float32
        ).astype(jnp.bfloat16)
        row_block = jnp.where(cols_right[None, :], upper_rows, top_rows)
        update = jnp.where(cols_right[None, :], row_block, jnp.zeros_like(row_block))
        root_col = step_index % pcol_count
        panel_local = step_index // pcol_count
        below_rows = rows_global >= past_row
        panel_raw = local_tile[:, panel_local * block_size : (panel_local + 1) * block_size]
        is_root = pcol_index == root_col

        def compute():
            product = jnp.dot(
                panel_raw, upper_inverse[step_index], preferred_element_type=jnp.float32
            ).astype(jnp.bfloat16)
            return jnp.where(below_rows[:, None], product, jnp.zeros_like(product))

        def nothing():
            return jnp.zeros_like(panel_raw)

        factor = from_root(lax.cond(is_root, compute, nothing), "pcol", root_col)
        local_tile = (
            local_tile.astype(jnp.float32)
            - jnp.dot(factor, update, preferred_element_type=jnp.float32)
        ).astype(jnp.bfloat16)
        updated_slab = local_tile[:, panel_local * block_size : (panel_local + 1) * block_size]
        stored = jnp.where(below_rows[:, None] & is_root, factor, updated_slab)
        local_tile = local_tile.at[
            :, panel_local * block_size : (panel_local + 1) * block_size
        ].set(stored)
        is_diag = prow_index == diag_row
        current = local_tile[diag_local * block_size : (diag_local + 1) * block_size]
        local_tile = local_tile.at[diag_local * block_size : (diag_local + 1) * block_size].set(
            jnp.where(is_diag, row_block, current)
        )
    return local_tile.reshape(shape_in)


def solution(mesh):
    return jax.shard_map(
        per_device,
        mesh=mesh,
        in_specs=(P(None, "prow", None, None, "pcol", None), P(), P(), P()),
        out_specs=P(None, "prow", None, None, "pcol", None),
        check_vma=False,
    )
```

profile of v0, /device:TPU:8, one launch (start us, length us, event | category | flops | bytes accessed | tf_op | source)
XLA Modules:
  0.0 652.1 jit_solution(6534921439675607615)
XLA Ops:
  6.5 0.8 fusion.64
  7.3 2.1 copy.57
  9.5 2.1 gather_fusion
  11.6 1.3 copy.37
  12.9 2.2 broadcast_select_fusion
  15.1 1.3 copy.58
  16.3 1.1 select_select_fusion.5
  17.8 2.6 copy.52
  20.6 0.3 reduce-window.48
  21.1 0.3 reduce-window.50
  21.7 0.3 reduce-window.34
  22.9 0.4 select_reduce_fusion.2
  23.3 0.7 fusion.9
  24.0 0.4 select_reduce_fusion.3
  24.4 1.0 select_reduce_fusion
  25.4 115.3 %all-reduce.13.cloned.1.call-done = (bf16[512,1024]{1,0:T(8,128)(2,1)}, bf16[512,1024]{0,1:T(8,128)(2,1)}) async-done(((bf16[512,1024]{1,0:T(8,128)(2,1)}, bf16[512,1024]{0,1:T(8,128)(2,1)}), (bf16[512,1024]{1,0:T(8,128)(2,1)}, bf16[512,1024]{0,1:T(8,128)(2,1)})) %all-reduce.13.cloned.1.call-update) | async-done | bytes 2097168 | tf_op jit(solution)/shard_map/psum | solution.py:11
  140.7 6.3 gather_fusion.1
  147.1 2.6 copy.38
  149.7 2.5 select_select_fusion.1
  152.1 7.0 %conditional.2 = (bf16[1024,512]{0,1:T(8,128)(2,1)S(1)}) conditional(s32[]{:T(128)} %convert_element_type.75, () %tuple.35, (pred[1024]{0:T(1024)(128)(4,1)S(1)}, bf16[2,512,512]{2,1,0:T(8,128)(2,1)}, bf16[1024,1024]{0,1:T(8,128)(2,1)S(1)}) %tuple.36), branch_computations={%region_11.14_spmd, %region_12.15_spmd} | conditional | flops 537919488 | bytes 13108260 | solution.py:85
  152.1 2.6 copy.39
  154.7 2.9 fusion
  157.6 1.5 copy.54
  159.1 1.0 broadcast_select_fusion.2
  160.4 0.7 compare_reduce_fusion.3
  161.1 2.4 fusion.11
  163.6 153.4 %all-reduce.7.cloned.1.call-done = bf16[1024,512]{0,1:T(8,128)(2,1)} async-done(((bf16[1024,512]{0,1:T(8,128)(2,1)}), bf16[1024,512]{0,1:T(8,128)(2,1)}) %all-reduce.7.cloned.1.call-update) | async-done | bytes 1048592 | tf_op jit(solution)/shard_map/psum | solution.py:11
  317.0 2.6 subtract_convert_fusion.1
  319.7 1.1 fusion.14
  320.8 1.7 broadcast_select_fusion.3
  322.5 1.3 copy-done
  323.9 2.9 copy.46
  326.7 2.1 gather_fusion.3
  328.8 0.5 copy.47
  329.3 1.1 select_select_fusion.4
  330.6 115.7 %all-reduce.11.cloned.1.call-done = (bf16[512,1024]{0,1:T(8,128)(2,1)}, bf16[512,1024]{0,1:T(8,128)(2,1)}) async-done(((bf16[512,1024]{0,1:T(8,128)(2,1)}, bf16[512,1024]{0,1:T(8,128)(2,1)}), (bf16[512,1024]{0,1:T(8,128)(2,1)}, bf16[512,1024]{0,1:T(8,128)(2,1)})) %all-reduce.11.cloned.1.call-update) | async-done | bytes 2097168 | tf_op jit(solution)/shard_map/psum | solution.py:11
  446.3 1.5 copy.42
  447.8 5.4 gather_fusion.2
  453.1 4.1 copy.43
  457.2 3.1 select_select_fusion
  460.5 1.1 broadcast_select_fusion.1
  461.7 2.6 fusion.13
  464.3 161.0 %all-reduce.9.cloned.1.call-done = bf16[1024,512]{0,1:T(8,128)(2,1)} async-done(((bf16[1024,512]{0,1:T(8,128)(2,1)}), bf16[1024,512]{0,1:T(8,128)(2,1)}) %all-reduce.9.cloned.1.call-update) | async-done | bytes 1048592 | tf_op jit(solution)/shard_map/psum | solution.py:11
  625.3 3.9 subtract_convert_fusion
  629.2 3.3 fusion.15
  632.5 2.5 fusion.16
  635.0 3.3 reshape.401
  638.3 7.3 %copy.49 = bf16[2,1,512,2,1,512]{5,3,4,2,1,0:T(2,128)(2,1)} copy(bf16[2,1,512,2,1,512]{2,0,5,3,4,1:T(2,128)(2,1)S(1)} %reshape.401) | data formatting | bytes 4194304 | tf_op jit(solution)/shard_map/reshape | solution.py:100
  (60 shorter events, 2.6 us)
Async XLA Ops:
  6.5 134.2 %all-reduce.13.cloned.1.call-start = ((), (), s32[]{:S(2)}) async-start(), calls=%async_computation.3 | async-start | bytes 4194304 | tf_op jit(solution)/shard_map/psum | solution.py:11
  12.9 3.4 copy-start.3
  16.3 1.2 copy-start.6
  17.5 299.5 %all-reduce.7.cloned.1.call-start = ((), (), s32[]{:S(2)}) async-start(), calls=%async_computation | async-start | bytes 2097152 | tf_op jit(solution)/shard_map/psum | solution.py:11
  152.1 2.6 copy-start.7
  160.2 286.1 %all-reduce.11.cloned.1.call-start = ((), (), s32[]{:S(2)}) async-start(), calls=%async_computation.2 | async-start | bytes 4194304 | tf_op jit(solution)/shard_map/psum | solution.py:11
  317.0 2.6 copy-start.4
  322.5 1.3 copy-start
  330.5 294.8 %all-reduce.9.cloned.1.call-start = ((), (), s32[]{:S(2)}) async-start(), calls=%async_computation.1 | async-start | bytes 2097152 | tf_op jit(solution)/shard_map/psum | solution.py:11
  453.1 4.1 copy-start.1
  461.6 163.7 %copy-start.2 = (bf16[1024,1024]{0,1:T(8,128)(2,1)S(1)}, bf16[1024,1024]{0,1:T(8,128)(2,1)}, u32[]{:S(2)}) copy-start(bf16[1024,1024]{0,1:T(8,128)(2,1)} %select_select_fusion) | copy-start | bytes 6291460
  625.3 3.9 copy-start.5
Sparse Core Ops, SparseCore 0:
  17.6 123.0 all-reduce.12
  160.3 156.6 all-reduce.6
  330.6 115.6 all-reduce.10
  461.8 163.4 all-reduce.8
where the time goes:
time: 653 us; the launch traced here: 652 us
  waiting for transfers between devices  546 us (84%)
  local copies, waits for them, and re-layouts  52.3 us (8%)
  other arithmetic  26 us (4%)
  matrix products  14.5 us (2%)
  between operations  13.4 us (2%)
    psum x4, waiting for transfers between devices, from_root(): return lax.psum(jnp.where(mine, value, jnp.zeros_like(value)), axis)  545 us
    gather x4, local copies, waits for them, and re-layouts, per_device(): jnp.take(old_top, giver_row, axis=0)  18.4 us
  transfers between devices with their start and end apart: 4, of which 4 were waited for; matrix products, arithmetic and copies ran while one was open for 2% of the time, Pallas kernels for 0%

commit v1 on v0

--- a/solution.py
+++ b/solution.py
@@ -8,7 +8,7 @@
 
 def from_root(value, axis, root):
     mine = lax.axis_index(axis) == root
-    return lax.psum(jnp.where(mine, value, jnp.zeros_like(value)), axis)
+    return jnp.sum(lax.all_gather(jnp.where(mine, value, jnp.zeros_like(value)), axis), axis=0)
 
 
 def pairing(sources, first_row, panel_width):

time: 653 us -> 995 us (1.52)
  the two profiles are of different devices: /device:TPU:8 before, /device:TPU:1 now
where the time goes in v1:
time: 995 us; the launch traced here: 994 us
  waiting for transfers between devices  835 us (84%)
  other arithmetic  70.2 us (7%)
  local copies, waits for them, and re-layouts  57.7 us (6%)
  matrix products  16.9 us (2%)
  between operations  13.7 us (1%)
    all_gather x4, waiting for transfers between devices, from_root(): lax.all_gather(jnp.where(mine, value, jnp.zeros_like(value)), axis)  656 us
    psum x2, waiting for transfers between devices, per_device(): lax.psum(contrib, 'prow').astype(jnp.float32).astype(jnp.bfloat16)  179 us
    reduce_sum x4, other arithmetic, from_root(): jnp.sum(lax.all_gather(jnp.where(mine, value, jnp.zeros_like(value)), axi...  40.4 us
  transfers between devices with their start and end apart: 6, of which 6 were waited for; matrix products, arithmetic and copies ran while one was open for 9% of the time, Pallas kernels for 0%

profile of v1, /device:TPU:1, one launch (start us, length us, event | category | flops | bytes accessed | tf_op | source)
XLA Modules:
  0.0 994.0 jit_solution(323099062400877377)
XLA Ops:
  6.5 2.1 broadcast_select_fusion
  8.6 1.6 select_n.235
  10.3 2.2 copy.62
  12.5 2.1 gather_fusion
  14.6 1.3 copy.46
  15.9 2.3 select_select_fusion.5
  21.9 0.7 fusion.9
  22.6 1.0 select_reduce_fusion
  23.6 2.6 copy.61
  26.2 87.8 %all-gather.8.cloned.1.call-done = bf16[16,512,1024]{2,1,0:T(8,128)(2,1)} async-done(((bf16[1,512,1024]{2,1,0:T(8,128)(2,1)}), bf16[16,512,1024]{2,1,0:T(8,128)(2,1)}) %all-gather.8.cloned.1.call-update) | async-done | bytes 16777232 | tf_op jit(solution)/shard_map/all_gather | solution.py:11
  114.0 9.3 reduce_sum.84
  123.3 4.1 gather_fusion.1
  127.4 2.6 copy.47
  130.0 2.5 select_select_fusion.1
  132.4 4.6 conditional.2
  132.5 2.6 copy.48
  135.0 2.1 fusion
  137.1 1.0 broadcast_select_fusion.2
  138.4 0.6 compare_reduce_fusion.3
  139.1 92.5 %all-reduce.3.cloned.1.call-done = bf16[512,1024]{0,1:T(8,128)(2,1)} async-done(((bf16[512,1024]{0,1:T(8,128)(2,1)}), bf16[512,1024]{0,1:T(8,128)(2,1)}) %all-reduce.3.cloned.1.call-update) | async-done | bytes 1048592 | tf_op jit(solution)/shard_map/psum | solution.py:64
  231.6 3.5 fusion.11
  235.0 240.3 %all-gather.10.cloned.1.call-done = bf16[32768,512]{1,0:T(8,128)(2,1)} async-done(((bf16[1024,512]{1,0:T(8,128)(2,1)}), bf16[32768,512]{1,0:T(8,128)(2,1)}) %all-gather.10.cloned.1.call-update) | async-done | bytes 33554448 | tf_op jit(solution)/shard_map/all_gather | solution.py:11
  475.4 11.4 %reduce_sum.87 = bf16[1024,512]{1,0:T(8,128)(2,1)S(1)} reduce(bf16[32,1024,512]{2,1,0:T(8,128)(2,1)} %bitcast.57, bf16[]{:T(256)} %constant.279.clone.1), dimensions={0}, to_apply=%region_13.16 | reduce | flops 16252928 | bytes 34603008 | tf_op jit(solution)/shard_map/reduce_sum | solution.py:11
  486.8 1.3 copy.50
  488.1 4.0 subtract_convert_fusion.1
  492.1 3.3 fusion.14
  495.4 2.9 broadcast_select_fusion.3
  498.4 2.9 copy.54
  501.3 2.1 gather_fusion.3
  503.3 0.5 copy.55
  503.9 1.1 select_select_fusion.4
  505.1 88.4 %all-gather.12.cloned.1.call-done = bf16[8192,1024]{0,1:T(8,128)(2,1)} async-done(((bf16[512,1024]{0,1:T(8,128)(2,1)}), bf16[8192,1024]{0,1:T(8,128)(2,1)}) %all-gather.12.cloned.1.call-update) | async-done | bytes 16777232 | tf_op jit(solution)/shard_map/all_gather | solution.py:11
  593.5 12.1 %copy.63 = bf16[128,8,16,512]{3,2,1,0:T(8,128)(2,1)S(1)} copy(bf16[128,8,16,512]{3,1,2,0:T(8,128)(2,1)} %bitcast.59) | data formatting | bytes 33554432
  605.6 8.2 bitcast_reduce_fusion
  614.4 4.1 gather_fusion.2
  618.4 2.6 copy.52
  621.0 2.5 select_select_fusion
  623.8 1.0 broadcast_select_fusion.1
  624.9 86.0 %all-reduce.5.cloned.1.call-done = bf16[512,1024]{0,1:T(8,128)(2,1)} async-done(((bf16[512,1024]{0,1:T(8,128)(2,1)}), bf16[512,1024]{0,1:T(8,128)(2,1)}) %all-reduce.5.cloned.1.call-update) | async-done | bytes 1048592 | tf_op jit(solution)/shard_map/psum | solution.py:64
  710.9 3.4 fusion.13
  714.4 239.7 %all-gather.14.cloned.1.call-done = bf16[32768,512]{1,0:T(8,128)(2,1)} async-done(((bf16[1024,512]{1,0:T(8,128)(2,1)}), bf16[32768,512]{1,0:T(8,128)(2,1)}) %all-gather.14.cloned.1.call-update) | async-done | bytes 33554448 | tf_op jit(solution)/shard_map/all_gather | solution.py:11
  954.1 11.4 %reduce_sum.91 = bf16[1024,512]{1,0:T(8,128)(2,1)S(1)} reduce(bf16[32,1024,512]{2,1,0:T(8,128)(2,1)} %bitcast.58, bf16[]{:T(256)} %constant.279.clone.1), dimensions={0}, to_apply=%region_25.28 | reduce | flops 16252928 | bytes 34603008 | tf_op jit(solution)/shard_map/reduce_sum | solution.py:11
  965.5 1.3 copy.57
  966.9 3.9 subtract_convert_fusion
  970.8 3.3 fusion.15
  974.1 2.5 fusion.16
  976.6 3.3 reshape.411
  979.9 7.3 copy.58
  (66 shorter events, 5.1 us)
Async XLA Ops:
  6.5 107.5 %all-gather.8.cloned.1.call-start = ((), (), s32[]{:S(2)}) async-start(), calls=%async_computation.1 | async-start | bytes 17825792 | tf_op jit(solution)/shard_map/all_gather | solution.py:11
  10.2 221.4 %all-reduce.3.cloned.1.call-start = ((), (), s32[]{:S(2)}) async-start(), calls=%async_computation | async-start | bytes 2097152 | tf_op jit(solution)/shard_map/psum | solution.py:64
  10.2 2.2 copy-start.4
  18.3 457.1 %all-gather.10.cloned.1.call-start = ((), (), s32[]{:S(2)}) async-start(), calls=%async_computation.3 | async-start | bytes 34603008 | tf_op jit(solution)/shard_map/all_gather | solution.py:11
  138.2 455.4 %all-gather.12.cloned.1.call-start = ((), (), s32[]{:S(2)}) async-start(), calls=%async_computation.4 | async-start | bytes 17825792 | tf_op jit(solution)/shard_map/all_gather | solution.py:11
  488.1 4.0 copy-start.1
  492.1 3.3 copy-start.2
  498.3 212.6 %all-reduce.5.cloned.1.call-start = ((), (), s32[]{:S(2)}) async-start(), calls=%async_computation.2 | async-start | bytes 2097152 | tf_op jit(solution)/shard_map/psum | solution.py:64
  505.0 449.1 %all-gather.14.cloned.1.call-start = ((), (), s32[]{:S(2)}) async-start(), calls=%async_computation.5 | async-start | bytes 34603008 | tf_op jit(solution)/shard_map/all_gather | solution.py:11
  966.9 3.9 copy-start
  970.8 3.3 copy-start.3
Sparse Core Ops, SparseCore 0:
  10.3 103.6 all-gather.7
  116.3 115.2 all-reduce.2
  235.2 240.0 all-gather.9
  498.4 95.0 all-gather.11
  595.8 115.1 all-reduce.4
  714.0 240.0 all-gather.13
